TPU v7x, 512 devices: a whole 4x4x16 slice. The times are simulated.
512 devices in a mesh: sample: 32 (over y, x, core), space: 16 (over z).
Axes of the slice: x: 4, y: 4, z: 16, core: 2. Of those that a mesh axis runs over, the one named last changes fastest.
Arguments:
- volumes: bfloat16 [32, 32, 64, 16, 128], P('sample', None, 'space'), may hold values from -360 to 360
- depth_kernel: float32 [32, 27], replicated, may hold values from -1.25 to 1.25
- point_weight: bfloat16 [32, 32], replicated, may hold values from -1 to 1
- cotangent: bfloat16 [32, 32, 64, 16, 128], P('sample', None, 'space'), may hold values from -4.1 to 4.1
Outputs:
- whitened: bfloat16 [32, 32, 64, 16, 128], P('sample', None, 'space')
- d_volumes: bfloat16 [32, 32, 64, 16, 128], P('sample', None, 'space')
- d_point: float32 [32, 32], replicated
- d_kernel: float32 [32, 27], replicated
All inputs are finite; a program needn't handle non-finite values.
Results may differ from a plain program's by a relative error of at most 0.0067.
Values may be sent and summed in bfloat16 or wider, within the bound.
No kernel may reach another device: no remote copies, remote signals or barrier semaphores. Data moves between devices by JAX's collectives and lax.ppermute only.
A program may use at most 64 MiB of HBM per device.

v0:
```python
from functools import partial
import math
import jax
import jax.numpy as jnp
from jax import lax
from jax.sharding import PartitionSpec as P

GSIZE = 16
NEWTON = 5
GROUPS = 2
epsilon = 1e-05
highest = lax.Precision.HIGHEST


def with_halo(block, sides, width):
    for axis, dim in sides:
        count = lax.axis_size(axis)
        forward = [(i, i + 1) for i in range(count - 1)]
        backward = [(target, source) for source, target in forward]
        low = lax.ppermute(
            lax.slice_in_dim(block, block.shape[dim] - width, None, axis=dim), axis, forward
        )
        high = lax.ppermute(lax.slice_in_dim(block, 0, width, axis=dim), axis, backward)
        block = jnp.concatenate([low, block, high], axis=dim)
    return block


def matmul_high(matrix, operand):
    return jnp.matmul(matrix, operand, precision=highest)


def contract_rows(matrix, operand):
    return jnp.einsum(
        "cv,dv->cd", matrix, operand, precision=highest, preferred_element_type=jnp.float32
    )


def contract_cols(matrix, operand):
    return jnp.einsum(
        "kc,kv->cv", matrix, operand, precision=highest, preferred_element_type=jnp.float32
    )


def block_diagonal(blocks):
    identity = jnp.eye(blocks.shape[0], dtype=blocks.dtype)
    full_size = blocks.shape[0] * blocks.shape[1]
    return jnp.einsum("gh,gij->gihj", identity, blocks, precision=highest).reshape(
        full_size, full_size
    )


def whiten_stats(first_sums, second_sums, voxel_count):
    groups = second_sums.shape[0]
    group_size = second_sums.shape[1]
    average = (first_sums / voxel_count).reshape(groups, group_size)
    identity = jnp.eye(group_size, dtype=second_sums.dtype)
    covariance = (
        second_sums / voxel_count - average[:, :, None] * average[:, None, :] + epsilon * identity
    )
    traces = jnp.trace(covariance, axis1=1, axis2=2)
    normed = covariance / traces[:, None, None]
    project = jnp.broadcast_to(identity, covariance.shape)
    for newton_step in range(NEWTON):
        cubed = matmul_high(matmul_high(project, project), project)
        project = 0.5 * (3.0 * project - matmul_high(cubed, normed))
    whiten_mat = project / jnp.sqrt(traces)[:, None, None]
    offset = jnp.einsum("gij,gj->gi", whiten_mat, average, precision=highest)
    return (whiten_mat, offset)


def adjoint_terms(pull_back, whiten_mat, grad_first, grad_second):
    d_first, d_second = pull_back(
        (grad_second, -grad_first.reshape(whiten_mat.shape[0], whiten_mat.shape[1]))
    )
    adjoint = block_diagonal(jnp.swapaxes(whiten_mat, 1, 2))
    symmetric = block_diagonal(d_second + jnp.swapaxes(d_second, 1, 2))
    return (d_first, adjoint, symmetric)


def gradient_signal(adjoint, d_first, symmetric, grad_part, mixed_part):
    first_term = jnp.dot(adjoint, grad_part, precision=highest, preferred_element_type=jnp.float32)
    third_term = jnp.dot(
        symmetric, mixed_part, precision=highest, preferred_element_type=jnp.float32
    )
    return first_term + d_first[:, None] + third_term


def pad_sides(extended):
    return jnp.pad(extended, ((0, 0), (0, 0), (1, 1), (1, 1)))


def tap_cells(padded, tap_index, depth_cells):
    plane_off = tap_index // 9
    row_off = tap_index // 3 % 3
    col_off = tap_index % 3
    height = padded.shape[2] - 2
    width_cells = padded.shape[3] - 2
    return padded[
        :,
        plane_off : plane_off + depth_cells,
        row_off : row_off + height,
        col_off : col_off + width_cells,
    ]


def depth_conv(extended, kernel, depth_cells):
    padded = pad_sides(extended)
    summed = jnp.zeros(
        (extended.shape[0], depth_cells, extended.shape[2], extended.shape[3]), jnp.float32
    )
    for tap_index in range(27):
        summed = summed + kernel[:, tap_index][:, None, None, None] * tap_cells(
            padded, tap_index, depth_cells
        ).astype(jnp.float32)
    return summed


def depth_adjoint(grad_ext, kernel, depth_cells):
    padded = pad_sides(grad_ext)
    height = grad_ext.shape[2]
    width_cells = grad_ext.shape[3]
    summed = jnp.zeros((grad_ext.shape[0], depth_cells, height, width_cells), jnp.float32)
    for tap_index in range(27):
        plane_off = 2 - tap_index // 9
        row_off = 2 - tap_index // 3 % 3
        col_off = 2 - tap_index % 3
        summed = (
            summed
            + kernel[:, tap_index][:, None, None, None]
            * padded[
                :,
                plane_off : plane_off + depth_cells,
                row_off : row_off + height,
                col_off : col_off + width_cells,
            ]
        )
    return summed


def on_device(volumes, depth_kernel, point_weight, cotangent):
    volume = volumes[0]
    grad_in = cotangent[0]
    channels, depth_cells, height, width_cells = volume.shape
    voxels = depth_cells * height * width_cells
    voxel_count = float(voxels * lax.axis_size("sample") * lax.axis_size("space"))
    grad_flat = grad_in.reshape(channels, voxels)
    extended = with_halo(volume, (("space", 1),), 1)
    hidden = (
        depth_conv(extended, depth_kernel, depth_cells)
        .astype(jnp.bfloat16)
        .reshape(channels, voxels)
    )
    mixed_out = jnp.dot(point_weight, hidden, preferred_element_type=jnp.float32).astype(
        jnp.bfloat16
    )
    grouped = mixed_out.reshape(GROUPS, GSIZE, voxels)
    local_first = jnp.sum(mixed_out.astype(jnp.float32), axis=1)
    local_second = jnp.einsum("giv,gjv->gij", grouped, grouped, preferred_element_type=jnp.float32)
    grad_first = jnp.sum(grad_flat.astype(jnp.float32), axis=1)
    grad_second = jnp.einsum(
        "giv,gjv->gij",
        grad_flat.reshape(GROUPS, GSIZE, voxels),
        grouped,
        preferred_element_type=jnp.float32,
    )
    padded_x = pad_sides(extended)
    weight_f = point_weight.astype(jnp.float32)
    stats_fn = partial(whiten_stats, voxel_count=voxel_count)
    first_sums, second_sums, grad_first, grad_second = lax.psum(
        (local_first, local_second, grad_first, grad_second), ("sample", "space")
    )
    (whiten_mat, offset), pull_back = jax.vjp(stats_fn, first_sums, second_sums)
    d_first, adjoint, symmetric = adjoint_terms(pull_back, whiten_mat, grad_first, grad_second)
    whitened = (
        jnp.dot(
            block_diagonal(whiten_mat),
            mixed_out,
            precision=highest,
            preferred_element_type=jnp.float32,
        )
        - offset.reshape(channels)[:, None]
    ).astype(jnp.bfloat16)
    d_mixed = gradient_signal(adjoint, d_first, symmetric, grad_flat, mixed_out)
    d_hidden = contract_cols(weight_f, d_mixed).reshape(channels, depth_cells, height, width_cells)
    grad_ext = with_halo(d_hidden, (("space", 1),), 1)
    kernel_terms = jnp.stack(
        [
            jnp.sum(
                d_hidden * tap_cells(padded_x, tap_index, depth_cells).astype(jnp.float32),
                axis=(1, 2, 3),
            )
            for tap_index in range(27)
        ],
        axis=1,
    )
    d_point, d_kernel = lax.psum(
        (contract_rows(d_mixed, hidden), kernel_terms), ("sample", "space")
    )
    d_volume = depth_adjoint(grad_ext, depth_kernel, depth_cells).astype(jnp.bfloat16)
    scale_out = 1.0 / math.sqrt(voxel_count)
    return (
        whitened.reshape(1, channels, depth_cells, height, width_cells),
        d_volume[None],
        d_point * scale_out,
        d_kernel * scale_out,
    )


def solution(mesh):
    in_specs = (
        P("sample", None, "space", None, None),
        P(),
        P(),
        P("sample", None, "space", None, None),
    )
    out_specs = (
        P("sample", None, "space", None, None),
        P("sample", None, "space", None, None),
        P(),
        P(),
    )
    return jax.shard_map(
        on_device, mesh=mesh, in_specs=in_specs, out_specs=out_specs, check_vma=False
    )
```

profile of v0, /device:TPU:1, one launch (start us, length us, event | category | flops | bytes accessed | tf_op | source)
XLA Modules:
  0.0 388.2 jit_solution(1286581559153312555)
XLA Ops:
  1.8 4.4 %collective-permute-start = (bf16[32,1,16,128]{3,2,1,0:T(8,128)(2,1)S(1)}, bf16[32,1,16,128]{3,2,1,0:T(8,128)(2,1)S(1)}, u32[]{:S(2)}, u32[]{:S(2)}) collective-permute-start(bf16[32,1,16,128]{3,2,1,0:T(8,128)(2,1)S(1)} %get-tuple-element.77), channel_id=1, source_target_pairs={{0,1},{1,2},{2,3},{3,4},{4,5},{5,6},{6,7},{7,8},{8,9},{9,10},{10,1... | collective-permute-start | bytes 393224 | tf_op jit(solution)/shard_map/ppermute | solution.py:20
  9.2 1.9 slice_reduce_fusion.25
  11.1 2.6 slice_reduce_fusion.26
  13.7 2.1 reshape_squeeze.3
  15.8 2.1 reshape_reshape_squeeze.3
  17.8 2.2 reshape.120
  22.5 3.0 select_maximum_fusion.2
  25.5 7.8 %fusion.59 = bf16[32,4,16,128]{3,2,1,0:T(8,128)(2,1)S(1)} fusion(bf16[32,4,16,128]{3,2,1,0:T(8,128)(2,1)S(1)} %bitcast.174, bf16[32,1,16,128]{3,2,1,0:T(8,128)(2,1)} %collective-permute-done.1, bf16[32,1,16,128]{3,2,1,0:T(8,128)(2,1)S(1)} %collective-permute-done, f32[32]{0:T(128)} %get-tuple-element.67, f32[32]{0:T(128)} %get-tuple-element.68, ...), kind=kLoop, calls=%fused_computation.140 | loop fusion | flops 21757952 | bytes 13897088 | tf_op jit(solution)/shard_map/convert_element_type | solution.py:150
  36.4 111.9 %all-reduce.3 = (f32[32]{0:T(128)}, f32[2,16,16]{2,1,0:T(8,128)}, f32[2,16,16]{1,2,0:T(8,128)}, f32[32]{0:T(128)}) all-reduce(f32[32]{0:T(128)} %get-tuple-element.91, f32[2,16,16]{2,1,0:T(8,128)} %fusion.215, f32[2,16,16]{1,2,0:T(8,128)} %convolution_bitcast_fusion, ...), channel_id=1, replica_groups=mesh['sample'=32,'space'=16] {'sample','space'}, use_global_device_ids=true, to_apply=%region_2.3 | all-reduce | flops 1088 | bytes 8704 | tf_op jit(solution)/shard_map/psum | solution.py:169
  162.7 1.6 fusion.212
  168.7 1.5 fusion.211
  174.2 1.5 fusion.210
  179.6 1.5 fusion.209
  198.2 1.6 fusion.208
  205.4 1.6 multiply_reduce_fusion.2
  209.7 1.5 multiply_reduce_fusion.3
  214.2 1.4 multiply_reduce_fusion.1
  218.5 1.5 multiply_bitcast_fusion
  220.0 1.4 reshape.118
  221.4 1.4 reshape.117
  222.9 1.7 convolution_add_fusion.1
  225.9 1.5 fusion.91
  228.9 6.7 %fusion.60 = (f32[32]{0:T(128)S(1)}, f32[32]{0:T(128)S(1)}, f32[32]{0:T(128)}, f32[32]{0:T(128)}, f32[32]{0:T(128)}, /*index=5*/f32[32]{0:T(128)}, f32[32]{0:T(1...) fusion(f32[32,4,16,128]{3,2,1,0:T(8,128)S(1)} %bitcast.164, ...), kind=kLoop, calls=%fused_computation.141 | loop fusion | flops 14155200 | bytes 10488064 | tf_op jit(solution)/shard_map/reduce_sum | solution.py:188
  238.4 1.4 reshape.115
  239.8 4.3 %fusion.57 = (f32[32]{0:T(128)}, f32[32]{0:T(128)}, f32[32]{0:T(128)}, f32[32]{0:T(128)}, f32[32]{0:T(128)}, /*index=5*/f32[32]{0:T(128)}, f32[32]{0:T(128)}, f32[32]{0:T(128)}) fusion(f32[32,4,16,128]{3,2,1,0:T(8,128)S(1)} %bitcast.166, bf16[32,6,18,130]{3,2,1,0:T(8,128)(2,1)S(1)} %select_maximum_fusion.2, bf16[32,4,16,128]{3,2,1,0:T(8,128)(2,1)} %bitcast.172, ...), kind=kLoop, calls=%fused_computation.138 | loop fusion | flops 6815488 | bytes 4981760 | tf_op jit(solution)/shard_map/reduce_sum | solution.py:188
  244.4 2.8 stack.111
  247.2 99.9 %all-reduce.2 = (f32[32,32]{1,0:T(8,128)S(1)}, f32[32,27]{0,1:T(8,128)S(1)}) all-reduce(f32[32,32]{1,0:T(8,128)} %fusion.91, f32[32,27]{0,1:T(8,128)S(1)} %stack.111), channel_id=1, replica_groups=mesh['sample'=32,'space'=16] {'sample','space'}, use_global_device_ids=true, to_apply=%region_11.12 | all-reduce | flops 1888 | bytes 15104 | tf_op jit(solution)/shard_map/psum | solution.py:196
  347.1 3.3 collective-permute-start.2
  351.6 1.6 fusion.5
  355.6 3.7 collective-permute-done.3
  359.3 3.4 select_maximum_fusion
  363.0 25.1 %fusion.94 = bf16[1,32,4,16,128]{4,3,2,1,0:T(8,128)(2,1)} fusion(f32[32,6,18,130]{3,2,1,0:T(8,128)} %select_maximum_fusion, f32[32]{0:T(128)S(1)} %copy-done.23, f32[32]{0:T(128)S(1)} %copy-done.24, f32[32]{0:T(128)S(1)} %copy-done.26, f32[32]{0:T(128)S(1)} %copy-done.27, f32[32,4,16,128]{3,2,1,0:T(8,128)S(1)} %bitcast.168, ...), kind=kLoop, calls=%fused_computation.206 | loop fusion | flops 14680064 | bytes 27266432 | tf_op jit(solution)/shard_map/broadcast_in_dim | solution.py:203
  (180 shorter events, 76.9 us)
Async XLA Ops:
  1.8 20.8 %collective-permute-start = (bf16[32,1,16,128]{3,2,1,0:T(8,128)(2,1)S(1)}, bf16[32,1,16,128]{3,2,1,0:T(8,128)(2,1)S(1)}, u32[]{:S(2)}, u32[]{:S(2)}) collective-permute-start(bf16[32,1,16,128]{3,2,1,0:T(8,128)(2,1)S(1)} %get-tuple-element.77), channel_id=1, source_target_pairs={{0,1},{1,2},{2,3},{3,4},{4,5},{5,6},{6,7},{7,8},{8,9},{9,10},{10,1... | collective-permute-start | bytes 393224 | tf_op jit(solution)/shard_map/ppermute | solution.py:20
  6.1 16.4 %collective-permute-start.1 = (bf16[32,1,16,128]{3,2,1,0:T(8,128)(2,1)S(1)}, bf16[32,1,16,128]{3,2,1,0:T(8,128)(2,1)}, u32[]{:S(2)}, u32[]{:S(2)}) collective-permute-start(bf16[32,1,16,128]{3,2,1,0:T(8,128)(2,1)S(1)} %get-tuple-element.78), channel_id=1, source_target_pairs={{1,0},{2,1},{3,2},{4,3},{5,4},{6,5},{7,6},{8,7},{9,8},{10,9},{11,1... | collective-permute-start | bytes 393224 | tf_op jit(solution)/shard_map/ppermute | solution.py:23
  34.5 191.4 %copy-start.1 = (bf16[8192,32]{0,1:T(8,128)(2,1)}, bf16[8192,32]{0,1:T(8,128)(2,1)S(1)}, u32[]{:S(2)}) copy-start(bf16[8192,32]{0,1:T(8,128)(2,1)S(1)} %get-tuple-element.92) | copy-start | bytes 1572868
  244.2 118.6 %copy-start.17 = (f32[32]{0:T(128)S(1)}, f32[32]{0:T(128)}, u32[]{:S(2)}) copy-start(f32[32]{0:T(128)} %get-tuple-element.61) | copy-start | bytes 388
  244.2 118.6 %copy-start.18 = (f32[32]{0:T(128)S(1)}, f32[32]{0:T(128)}, u32[]{:S(2)}) copy-start(f32[32]{0:T(128)} %get-tuple-element.62) | copy-start | bytes 388
  244.2 118.6 %copy-start.19 = (f32[32]{0:T(128)S(1)}, f32[32]{0:T(128)}, u32[]{:S(2)}) copy-start(f32[32]{0:T(128)} %get-tuple-element.63) | copy-start | bytes 388
  244.2 118.6 %copy-start.20 = (f32[32]{0:T(128)S(1)}, f32[32]{0:T(128)}, u32[]{:S(2)}) copy-start(f32[32]{0:T(128)} %get-tuple-element.64) | copy-start | bytes 388
  244.2 118.6 %copy-start.21 = (f32[32]{0:T(128)S(1)}, f32[32]{0:T(128)}, u32[]{:S(2)}) copy-start(f32[32]{0:T(128)} %get-tuple-element.65) | copy-start | bytes 388
  244.2 118.6 %copy-start.22 = (f32[32]{0:T(128)S(1)}, f32[32]{0:T(128)}, u32[]{:S(2)}) copy-start(f32[32]{0:T(128)} %get-tuple-element.66) | copy-start | bytes 388
  244.2 118.6 %copy-start.23 = (f32[32]{0:T(128)S(1)}, f32[32]{0:T(128)}, u32[]{:S(2)}) copy-start(f32[32]{0:T(128)} %get-tuple-element.67) | copy-start | bytes 388
  244.2 118.6 %copy-start.24 = (f32[32]{0:T(128)S(1)}, f32[32]{0:T(128)}, u32[]{:S(2)}) copy-start(f32[32]{0:T(128)} %get-tuple-element.68) | copy-start | bytes 388
  244.2 118.6 %copy-start.25 = (f32[32]{0:T(128)S(1)}, f32[32]{0:T(128)}, u32[]{:S(2)}) copy-start(f32[32]{0:T(128)} %get-tuple-element.42) | copy-start | bytes 388
  244.2 118.6 %copy-start.26 = (f32[32]{0:T(128)S(1)}, f32[32]{0:T(128)}, u32[]{:S(2)}) copy-start(f32[32]{0:T(128)} %get-tuple-element.43) | copy-start | bytes 388
  244.2 118.6 %copy-start.27 = (f32[32]{0:T(128)S(1)}, f32[32]{0:T(128)}, u32[]{:S(2)}) copy-start(f32[32]{0:T(128)} %get-tuple-element.44) | copy-start | bytes 388
  244.2 118.6 %copy-start.28 = (f32[32]{0:T(128)S(1)}, f32[32]{0:T(128)}, u32[]{:S(2)}) copy-start(f32[32]{0:T(128)} %get-tuple-element.45) | copy-start | bytes 388
  244.3 118.6 %copy-start.29 = (f32[32]{0:T(128)S(1)}, f32[32]{0:T(128)}, u32[]{:S(2)}) copy-start(f32[32]{0:T(128)} %get-tuple-element.46) | copy-start | bytes 388
  244.3 118.6 %copy-start.30 = (f32[32]{0:T(128)S(1)}, f32[32]{0:T(128)}, u32[]{:S(2)}) copy-start(f32[32]{0:T(128)} %get-tuple-element.47) | copy-start | bytes 388
  244.3 118.6 %copy-start.31 = (f32[32]{0:T(128)S(1)}, f32[32]{0:T(128)}, u32[]{:S(2)}) copy-start(f32[32]{0:T(128)} %get-tuple-element.48) | copy-start | bytes 388
  244.3 118.6 %copy-start.32 = (f32[32]{0:T(128)S(1)}, f32[32]{0:T(128)}, u32[]{:S(2)}) copy-start(f32[32]{0:T(128)} %get-tuple-element.49) | copy-start | bytes 388
  244.3 118.6 %copy-start.33 = (f32[32]{0:T(128)S(1)}, f32[32]{0:T(128)}, u32[]{:S(2)}) copy-start(f32[32]{0:T(128)} %get-tuple-element.50) | copy-start | bytes 388
  244.3 118.6 %copy-start.34 = (f32[32]{0:T(128)S(1)}, f32[32]{0:T(128)}, u32[]{:S(2)}) copy-start(f32[32]{0:T(128)} %get-tuple-element.51) | copy-start | bytes 388
  244.3 118.6 %copy-start.35 = (f32[32]{0:T(128)S(1)}, f32[32]{0:T(128)}, u32[]{:S(2)}) copy-start(f32[32]{0:T(128)} %get-tuple-element.52) | copy-start | bytes 388
  244.3 118.6 %copy-start.36 = (f32[32]{0:T(128)S(1)}, f32[32]{0:T(128)}, u32[]{:S(2)}) copy-start(f32[32]{0:T(128)} %get-tuple-element.53) | copy-start | bytes 388
  244.3 118.6 %copy-start.37 = (f32[32]{0:T(128)S(1)}, f32[32]{0:T(128)}, u32[]{:S(2)}) copy-start(f32[32]{0:T(128)} %get-tuple-element.54) | copy-start | bytes 388
  244.3 118.6 %copy-start.38 = (f32[32]{0:T(128)S(1)}, f32[32]{0:T(128)}, u32[]{:S(2)}) copy-start(f32[32]{0:T(128)} %get-tuple-element.55) | copy-start | bytes 388
  244.4 118.6 %copy-start.39 = (f32[32]{0:T(128)S(1)}, f32[32]{0:T(128)}, u32[]{:S(2)}) copy-start(f32[32]{0:T(128)} %get-tuple-element.56) | copy-start | bytes 388
  244.4 118.6 %copy-start.40 = (f32[32]{0:T(128)S(1)}, f32[32]{0:T(128)}, u32[]{:S(2)}) copy-start(f32[32]{0:T(128)} %get-tuple-element.57) | copy-start | bytes 388
  244.4 118.6 %copy-start.41 = (f32[32]{0:T(128)S(1)}, f32[32]{0:T(128)}, u32[]{:S(2)}) copy-start(f32[32]{0:T(128)} %get-tuple-element.58) | copy-start | bytes 388
  244.4 118.6 %copy-start.42 = (f32[32]{0:T(128)S(1)}, f32[32]{0:T(128)}, u32[]{:S(2)}) copy-start(f32[32]{0:T(128)} %get-tuple-element.59) | copy-start | bytes 388
  244.4 118.6 %copy-start.43 = (f32[32]{0:T(128)S(1)}, f32[32]{0:T(128)}, u32[]{:S(2)}) copy-start(f32[32]{0:T(128)} %get-tuple-element.60) | copy-start | bytes 388
  347.1 8.5 %collective-permute-start.2 = (f32[32,1,16,128]{3,2,1,0:T(8,128)}, f32[32,1,16,128]{3,2,1,0:T(8,128)S(1)}, u32[]{:S(2)}, u32[]{:S(2)}) collective-permute-start(f32[32,1,16,128]{3,2,1,0:T(8,128)} %get-tuple-element.75), channel_id=1, source_target_pairs={{0,1},{1,2},{2,3},{3,4},{4,5},{5,6},{6,7},{7,8},{8,9},{9,10},{10,1... | collective-permute-start | bytes 786440 | tf_op jit(solution)/shard_map/ppermute | solution.py:20
  350.3 9.0 %collective-permute-start.3 = (f32[32,1,16,128]{3,2,1,0:T(8,128)}, f32[32,1,16,128]{3,2,1,0:T(8,128)S(1)}, u32[]{:S(2)}, u32[]{:S(2)}) collective-permute-start(f32[32,1,16,128]{3,2,1,0:T(8,128)} %get-tuple-element.76), channel_id=1, source_target_pairs={{1,0},{2,1},{3,2},{4,3},{5,4},{6,5},{7,6},{8,7},{9,8},{10,9},{11,1... | collective-permute-start | bytes 786440 | tf_op jit(solution)/shard_map/ppermute | solution.py:23
  (17 other events, 113.1 us)
where the time goes:
time: 394 us; the launch traced here: 388 us
  blocking collectives  212 us (54%)
  other arithmetic  67.2 us (17%)
  local copies, waits for them, and re-layouts  48.5 us (12%)
  matrix products  45.2 us (11%)
  starting transfers between devices  10.2 us (3%)
    psum x1, blocking collectives, on_device(): lax.psum((local_first, local_second, grad_first, grad_second), ('sample',...  112 us
    psum x1, blocking collectives, on_device(): lax.psum((contract_rows(d_mixed, hidden), kernel_terms), ('sample', 'spac...  99.9 us
    dot_general x40, matrix products, matmul_high(): return jnp.matmul(matrix, operand, precision=highest)  33.2 us
    broadcast_in_dim x1, other arithmetic, on_device(): d_volume[None]  25.1 us
    reduce_sum x2, other arithmetic, on_device(): jnp.sum(d_hidden * tap_cells(padded_x, tap_index, depth_cells).astype(jnp...  11 us
  transfers between devices with their start and end apart: 4, of which 2 were waited for; matrix products, arithmetic and copies ran while one was open for 5% of the time, Pallas kernels for 0%

commit v1 on v0

--- a/solution.py
+++ b/solution.py
@@ -10,6 +10,7 @@
 GROUPS = 2
 epsilon = 1e-05
 highest = lax.Precision.HIGHEST
+lead_inputs = lambda point: lax.psum(lax.psum(point, "space"), axis_name="sample")
 
 
 def with_halo(block, sides, width):
@@ -166,8 +167,8 @@
     padded_x = pad_sides(extended)
     weight_f = point_weight.astype(jnp.float32)
     stats_fn = partial(whiten_stats, voxel_count=voxel_count)
-    first_sums, second_sums, grad_first, grad_second = lax.psum(
-        (local_first, local_second, grad_first, grad_second), ("sample", "space")
+    first_sums, second_sums, grad_first, grad_second = lead_inputs(
+        (local_first, local_second, grad_first, grad_second)
     )
     (whiten_mat, offset), pull_back = jax.vjp(stats_fn, first_sums, second_sums)
     d_first, adjoint, symmetric = adjoint_terms(pull_back, whiten_mat, grad_first, grad_second)

time: 394 us -> 470 us (1.19)
  blocking collectives: 212 us -> 287 us
    psum x1 -> x2, blocking collectives: 112 us -> 184 us  [the longest x1 134 us: lax.psum(lax.psum(point, 'space'), axis_name='sample')]
  transfers between devices with their start and end apart: 4 -> 4, of which waited for: 2 -> 2; matrix products, arithmetic and copies ran while one was open for 5% -> 4% of each run, Pallas kernels for 0% -> 0%
where the time goes in v1:
time: 470 us; the launch traced here: 464 us
  blocking collectives  287 us (61%)
  other arithmetic  67.1 us (14%)
  local copies, waits for them, and re-layouts  48.5 us (10%)
  matrix products  45.2 us (10%)
  starting transfers between devices  10.6 us (2%)
    psum x1, blocking collectives, lax.psum(lax.psum(point, 'space'), axis_name='sample')  134 us
    psum x1, blocking collectives, on_device(): lax.psum((contract_rows(d_mixed, hidden), kernel_terms), ('sample', 'spac...  103 us
    psum x1, blocking collectives, lax.psum(point, 'space')  50.6 us
    dot_general x40, matrix products, matmul_high(): return jnp.matmul(matrix, operand, precision=highest)  33.2 us
    broadcast_in_dim x1, other arithmetic, on_device(): d_volume[None]  25.1 us
    reduce_sum x2, other arithmetic, on_device(): jnp.sum(d_hidden * tap_cells(padded_x, tap_index, depth_cells).astype(jnp...  10.8 us
  transfers between devices with their start and end apart: 4, of which 2 were waited for; matrix products, arithmetic and copies ran while one was open for 4% of the time, Pallas kernels for 0%

profile of v1, /device:TPU:1, one launch (start us, length us, event | category | flops | bytes accessed | tf_op | source)
XLA Modules:
  0.0 463.5 jit_solution(4232659392136418412)
XLA Ops:
  1.8 4.4 collective-permute-start
  9.2 1.9 slice_reduce_fusion.25
  11.1 2.6 slice_reduce_fusion.26
  13.7 2.1 reshape_squeeze.3
  15.8 2.1 reshape_reshape_squeeze.3
  17.8 2.2 reshape.120
  22.5 3.0 select_maximum_fusion.2
  25.5 7.8 %fusion.59 = bf16[32,4,16,128]{3,2,1,0:T(8,128)(2,1)S(1)} fusion(bf16[32,4,16,128]{3,2,1,0:T(8,128)(2,1)S(1)} %bitcast.174, bf16[32,1,16,128]{3,2,1,0:T(8,128)(2,1)} %collective-permute-done.1, bf16[32,1,16,128]{3,2,1,0:T(8,128)(2,1)S(1)} %collective-permute-done, f32[32]{0:T(128)} %get-tuple-element.67, f32[32]{0:T(128)} %get-tuple-element.68, ...), kind=kLoop, calls=%fused_computation.140 | loop fusion | flops 21757952 | bytes 13897088 | tf_op jit(solution)/shard_map/convert_element_type | solution.py:151
  36.4 50.6 %all-reduce.4 = (f32[32]{0:T(128)}, f32[2,16,16]{2,1,0:T(8,128)}, f32[2,16,16]{1,2,0:T(8,128)}, f32[32]{0:T(128)}) all-reduce(f32[32]{0:T(128)} %get-tuple-element.95, f32[2,16,16]{2,1,0:T(8,128)} %fusion.215, f32[2,16,16]{1,2,0:T(8,128)} %convolution_bitcast_fusion, ...), channel_id=1, replica_groups=mesh['sample'=32,'space'=16] {'space'}, use_global_device_ids=true, to_apply=%region_3.4 | all-reduce | flops 1088 | bytes 8704 | tf_op jit(solution)/shard_map/psum | solution.py:13
  87.0 133.6 %all-reduce.3 = (f32[32]{0:T(128)}, f32[2,16,16]{2,1,0:T(8,128)}, f32[2,16,16]{1,2,0:T(8,128)}, f32[32]{0:T(128)}) all-reduce(f32[32]{0:T(128)} %get-tuple-element.75, f32[2,16,16]{2,1,0:T(8,128)} %get-tuple-element.76, f32[2,16,16]{1,2,0:T(8,128)} %get-tuple-element.77, ...), channel_id=1, replica_groups=mesh['sample'=32,'space'=16] {'sample'}, use_global_device_ids=true, to_apply=%region_4.5 | all-reduce | flops 1088 | bytes 8704 | tf_op jit(solution)/shard_map/psum | solution.py:13
  235.1 1.6 fusion.212
  241.1 1.5 fusion.211
  246.6 1.5 fusion.210
  252.1 1.5 fusion.209
  270.6 1.6 fusion.208
  277.8 1.6 multiply_reduce_fusion.2
  282.2 1.5 multiply_reduce_fusion.3
  291.0 1.5 multiply_bitcast_fusion
  292.4 1.4 reshape.118
  293.9 1.4 reshape.117
  295.3 1.7 convolution_add_fusion.1
  298.3 1.5 fusion.91
  301.4 6.5 %fusion.60 = (f32[32]{0:T(128)S(1)}, f32[32]{0:T(128)S(1)}, f32[32]{0:T(128)}, f32[32]{0:T(128)}, f32[32]{0:T(128)}, /*index=5*/f32[32]{0:T(128)}, f32[32]{0:T(1...) fusion(f32[32,4,16,128]{3,2,1,0:T(8,128)S(1)} %bitcast.164, ...), kind=kLoop, calls=%fused_computation.141 | loop fusion | flops 14155200 | bytes 10488064 | tf_op jit(solution)/shard_map/reduce_sum | solution.py:189
  310.6 1.4 reshape.115
  312.1 4.3 fusion.57
  316.6 2.8 stack.111
  319.4 102.5 %all-reduce.2 = (f32[32,32]{1,0:T(8,128)S(1)}, f32[32,27]{0,1:T(8,128)S(1)}) all-reduce(f32[32,32]{1,0:T(8,128)} %fusion.91, f32[32,27]{0,1:T(8,128)S(1)} %stack.111), channel_id=1, replica_groups=mesh['sample'=32,'space'=16] {'sample','space'}, use_global_device_ids=true, to_apply=%region_15.16 | all-reduce | flops 1888 | bytes 15104 | tf_op jit(solution)/shard_map/psum | solution.py:197
  422.0 3.7 collective-permute-start.2
  426.9 1.6 fusion.5
  430.9 3.7 collective-permute-done.3
  434.7 3.4 select_maximum_fusion
  438.3 25.1 %fusion.94 = bf16[1,32,4,16,128]{4,3,2,1,0:T(8,128)(2,1)} fusion(f32[32,6,18,130]{3,2,1,0:T(8,128)} %select_maximum_fusion, f32[32]{0:T(128)S(1)} %copy-done.23, f32[32]{0:T(128)S(1)} %copy-done.24, f32[32]{0:T(128)S(1)} %copy-done.26, f32[32]{0:T(128)S(1)} %copy-done.27, f32[32,4,16,128]{3,2,1,0:T(8,128)S(1)} %bitcast.168, ...), kind=kLoop, calls=%fused_computation.206 | loop fusion | flops 14680064 | bytes 27266432 | tf_op jit(solution)/shard_map/broadcast_in_dim | solution.py:204
  (181 shorter events, 78.5 us)
Async XLA Ops:
  1.8 20.8 %collective-permute-start = (bf16[32,1,16,128]{3,2,1,0:T(8,128)(2,1)S(1)}, bf16[32,1,16,128]{3,2,1,0:T(8,128)(2,1)S(1)}, u32[]{:S(2)}, u32[]{:S(2)}) collective-permute-start(bf16[32,1,16,128]{3,2,1,0:T(8,128)(2,1)S(1)} %get-tuple-element.81), channel_id=1, source_target_pairs={{0,1},{1,2},{2,3},{3,4},{4,5},{5,6},{6,7},{7,8},{8,9},{9,10},{10,1... | collective-permute-start | bytes 393224 | tf_op jit(solution)/shard_map/ppermute | solution.py:21
  6.1 16.4 %collective-permute-start.1 = (bf16[32,1,16,128]{3,2,1,0:T(8,128)(2,1)S(1)}, bf16[32,1,16,128]{3,2,1,0:T(8,128)(2,1)}, u32[]{:S(2)}, u32[]{:S(2)}) collective-permute-start(bf16[32,1,16,128]{3,2,1,0:T(8,128)(2,1)S(1)} %get-tuple-element.82), channel_id=1, source_target_pairs={{1,0},{2,1},{3,2},{4,3},{5,4},{6,5},{7,6},{8,7},{9,8},{10,9},{11,1... | collective-permute-start | bytes 393224 | tf_op jit(solution)/shard_map/ppermute | solution.py:24
  34.5 263.9 %copy-start.1 = (bf16[8192,32]{0,1:T(8,128)(2,1)}, bf16[8192,32]{0,1:T(8,128)(2,1)S(1)}, u32[]{:S(2)}) copy-start(bf16[8192,32]{0,1:T(8,128)(2,1)S(1)} %get-tuple-element.96) | copy-start | bytes 1572868
  316.4 121.6 %copy-start.17 = (f32[32]{0:T(128)S(1)}, f32[32]{0:T(128)}, u32[]{:S(2)}) copy-start(f32[32]{0:T(128)} %get-tuple-element.61) | copy-start | bytes 388
  316.4 121.6 %copy-start.18 = (f32[32]{0:T(128)S(1)}, f32[32]{0:T(128)}, u32[]{:S(2)}) copy-start(f32[32]{0:T(128)} %get-tuple-element.62) | copy-start | bytes 388
  316.4 121.6 %copy-start.19 = (f32[32]{0:T(128)S(1)}, f32[32]{0:T(128)}, u32[]{:S(2)}) copy-start(f32[32]{0:T(128)} %get-tuple-element.63) | copy-start | bytes 388
  316.4 121.6 %copy-start.20 = (f32[32]{0:T(128)S(1)}, f32[32]{0:T(128)}, u32[]{:S(2)}) copy-start(f32[32]{0:T(128)} %get-tuple-element.64) | copy-start | bytes 388
  316.4 121.6 %copy-start.21 = (f32[32]{0:T(128)S(1)}, f32[32]{0:T(128)}, u32[]{:S(2)}) copy-start(f32[32]{0:T(128)} %get-tuple-element.65) | copy-start | bytes 388
  316.4 121.6 %copy-start.22 = (f32[32]{0:T(128)S(1)}, f32[32]{0:T(128)}, u32[]{:S(2)}) copy-start(f32[32]{0:T(128)} %get-tuple-element.66) | copy-start | bytes 388
  316.4 121.6 %copy-start.23 = (f32[32]{0:T(128)S(1)}, f32[32]{0:T(128)}, u32[]{:S(2)}) copy-start(f32[32]{0:T(128)} %get-tuple-element.67) | copy-start | bytes 388
  316.4 121.6 %copy-start.24 = (f32[32]{0:T(128)S(1)}, f32[32]{0:T(128)}, u32[]{:S(2)}) copy-start(f32[32]{0:T(128)} %get-tuple-element.68) | copy-start | bytes 388
  316.4 121.6 %copy-start.25 = (f32[32]{0:T(128)S(1)}, f32[32]{0:T(128)}, u32[]{:S(2)}) copy-start(f32[32]{0:T(128)} %get-tuple-element.42) | copy-start | bytes 388
  316.5 121.6 %copy-start.26 = (f32[32]{0:T(128)S(1)}, f32[32]{0:T(128)}, u32[]{:S(2)}) copy-start(f32[32]{0:T(128)} %get-tuple-element.43) | copy-start | bytes 388
  316.5 121.6 %copy-start.27 = (f32[32]{0:T(128)S(1)}, f32[32]{0:T(128)}, u32[]{:S(2)}) copy-start(f32[32]{0:T(128)} %get-tuple-element.44) | copy-start | bytes 388
  316.5 121.6 %copy-start.28 = (f32[32]{0:T(128)S(1)}, f32[32]{0:T(128)}, u32[]{:S(2)}) copy-start(f32[32]{0:T(128)} %get-tuple-element.45) | copy-start | bytes 388
  316.5 121.6 %copy-start.29 = (f32[32]{0:T(128)S(1)}, f32[32]{0:T(128)}, u32[]{:S(2)}) copy-start(f32[32]{0:T(128)} %get-tuple-element.46) | copy-start | bytes 388
  316.5 121.6 %copy-start.30 = (f32[32]{0:T(128)S(1)}, f32[32]{0:T(128)}, u32[]{:S(2)}) copy-start(f32[32]{0:T(128)} %get-tuple-element.47) | copy-start | bytes 388
  316.5 121.6 %copy-start.31 = (f32[32]{0:T(128)S(1)}, f32[32]{0:T(128)}, u32[]{:S(2)}) copy-start(f32[32]{0:T(128)} %get-tuple-element.48) | copy-start | bytes 388
  316.5 121.6 %copy-start.32 = (f32[32]{0:T(128)S(1)}, f32[32]{0:T(128)}, u32[]{:S(2)}) copy-start(f32[32]{0:T(128)} %get-tuple-element.49) | copy-start | bytes 388
  316.5 121.6 %copy-start.33 = (f32[32]{0:T(128)S(1)}, f32[32]{0:T(128)}, u32[]{:S(2)}) copy-start(f32[32]{0:T(128)} %get-tuple-element.50) | copy-start | bytes 388
  316.5 121.6 %copy-start.34 = (f32[32]{0:T(128)S(1)}, f32[32]{0:T(128)}, u32[]{:S(2)}) copy-start(f32[32]{0:T(128)} %get-tuple-element.51) | copy-start | bytes 388
  316.5 121.6 %copy-start.35 = (f32[32]{0:T(128)S(1)}, f32[32]{0:T(128)}, u32[]{:S(2)}) copy-start(f32[32]{0:T(128)} %get-tuple-element.52) | copy-start | bytes 388
  316.6 121.6 %copy-start.36 = (f32[32]{0:T(128)S(1)}, f32[32]{0:T(128)}, u32[]{:S(2)}) copy-start(f32[32]{0:T(128)} %get-tuple-element.53) | copy-start | bytes 388
  316.6 121.6 %copy-start.37 = (f32[32]{0:T(128)S(1)}, f32[32]{0:T(128)}, u32[]{:S(2)}) copy-start(f32[32]{0:T(128)} %get-tuple-element.54) | copy-start | bytes 388
  316.6 121.6 %copy-start.38 = (f32[32]{0:T(128)S(1)}, f32[32]{0:T(128)}, u32[]{:S(2)}) copy-start(f32[32]{0:T(128)} %get-tuple-element.55) | copy-start | bytes 388
  316.6 121.6 %copy-start.39 = (f32[32]{0:T(128)S(1)}, f32[32]{0:T(128)}, u32[]{:S(2)}) copy-start(f32[32]{0:T(128)} %get-tuple-element.56) | copy-start | bytes 388
  316.6 121.6 %copy-start.40 = (f32[32]{0:T(128)S(1)}, f32[32]{0:T(128)}, u32[]{:S(2)}) copy-start(f32[32]{0:T(128)} %get-tuple-element.57) | copy-start | bytes 388
  316.6 121.6 %copy-start.41 = (f32[32]{0:T(128)S(1)}, f32[32]{0:T(128)}, u32[]{:S(2)}) copy-start(f32[32]{0:T(128)} %get-tuple-element.58) | copy-start | bytes 388
  316.6 121.6 %copy-start.42 = (f32[32]{0:T(128)S(1)}, f32[32]{0:T(128)}, u32[]{:S(2)}) copy-start(f32[32]{0:T(128)} %get-tuple-element.59) | copy-start | bytes 388
  316.6 121.6 %copy-start.43 = (f32[32]{0:T(128)S(1)}, f32[32]{0:T(128)}, u32[]{:S(2)}) copy-start(f32[32]{0:T(128)} %get-tuple-element.60) | copy-start | bytes 388
  422.0 9.0 %collective-permute-start.2 = (f32[32,1,16,128]{3,2,1,0:T(8,128)}, f32[32,1,16,128]{3,2,1,0:T(8,128)S(1)}, u32[]{:S(2)}, u32[]{:S(2)}) collective-permute-start(f32[32,1,16,128]{3,2,1,0:T(8,128)} %get-tuple-element.79), channel_id=1, source_target_pairs={{0,1},{1,2},{2,3},{3,4},{4,5},{5,6},{6,7},{7,8},{8,9},{9,10},{10,1... | collective-permute-start | bytes 786440 | tf_op jit(solution)/shard_map/ppermute | solution.py:21
  425.6 9.0 %collective-permute-start.3 = (f32[32,1,16,128]{3,2,1,0:T(8,128)}, f32[32,1,16,128]{3,2,1,0:T(8,128)S(1)}, u32[]{:S(2)}, u32[]{:S(2)}) collective-permute-start(f32[32,1,16,128]{3,2,1,0:T(8,128)} %get-tuple-element.80), channel_id=1, source_target_pairs={{1,0},{2,1},{3,2},{4,3},{5,4},{6,5},{7,6},{8,7},{9,8},{10,9},{11,1... | collective-permute-start | bytes 786440 | tf_op jit(solution)/shard_map/ppermute | solution.py:24
  (17 other events, 112.7 us)
